TPU v7x, 32 devices: a whole 2x2x4 slice. The times are simulated.
32 devices in a mesh: grp: 2 (over y), row: 4 (over x, core), col: 4 (over z).
Axes of the slice: x: 2, y: 2, z: 4, core: 2. Of those that a mesh axis runs over, the one named last changes fastest.
Arguments:
- amplitudes: bfloat16 [32768, 16384], P(('grp', 'row'), 'col'), parts along dimension 0, may hold values from -0.046875 to 0.046875
- cholesky: bfloat16 [1024, 32768], P('row', ('grp', 'col')), parts along dimension 1, may hold values from -1.078125 to 1.078125
- occ_index: int32 [32768], P('grp'), parts along dimension 0, may hold values from 0 to 31
- vir_index: int32 [32768], P('grp'), parts along dimension 0, may hold values from 0 to 511
- eps_occ: float32 [64], P('grp'), parts along dimension 0, may hold values from -2 to -0.3
- eps_vir: float32 [1024], P('grp'), parts along dimension 0, may hold values from 0.2 to 3
Outputs:
- new_amplitudes: bfloat16 [32768, 16384], P(('grp', 'row'), 'col'), parts along dimension 0
There are 2 independent parts, one for each index of `grp`. A program takes and returns all parts, laid end to end along the dimension named above; each array names one. Nothing has to cross between parts.
All inputs are finite; a program needn't handle non-finite values.
Results may differ from a plain program's by a relative error of at most 0.0056.
Values may be sent and summed in bfloat16 or wider, within the bound.
A program may use at most 128 MiB of HBM per device.

v0:
```python
import jax
import jax.numpy as jnp
from jax import lax
from jax.sharding import PartitionSpec as P


def pair_gaps(occ_index, vir_index, eps_occ, eps_vir, begin_pair, pair_count):
    occ_rows = lax.dynamic_slice_in_dim(occ_index, begin_pair, pair_count, 0)
    vir_rows = lax.dynamic_slice_in_dim(vir_index, begin_pair, pair_count, 0)
    occ_table = jnp.arange(eps_occ.shape[0], dtype=jnp.int32)
    vir_table = jnp.arange(eps_vir.shape[0], dtype=jnp.int32)
    occ_energy = jnp.sum(
        jnp.where(occ_rows[:, None] == occ_table[None, :], eps_occ[None, :], 0.0), axis=1
    )
    vir_energy = jnp.sum(
        jnp.where(vir_rows[:, None] == vir_table[None, :], eps_vir[None, :], 0.0), axis=1
    )
    return vir_energy - occ_energy


def local(amplitudes, cholesky, occ_index, vir_index, eps_occ, eps_vir):
    row_position = lax.axis_index("row")
    col_position = lax.axis_index("col")
    rows_block, cols_block = amplitudes.shape
    all_pairs = lax.all_gather(cholesky, "col", axis=1, tiled=True)
    chol_rows = lax.all_to_all(all_pairs, "row", split_axis=1, concat_axis=0, tiled=True)
    dressed = lax.psum_scatter(
        jnp.dot(chol_rows, amplitudes, preferred_element_type=jnp.float32),
        "row",
        scatter_dimension=0,
        tiled=True,
    )
    ydress = (cholesky.astype(jnp.float32) + dressed).astype(jnp.bfloat16)
    contract = (((0,), (0,)), ((), ()))
    ydress_pairs = lax.all_gather(ydress, "col", axis=1, tiled=True)
    ydress_rows = lax.all_to_all(ydress_pairs, "row", split_axis=1, concat_axis=0, tiled=True)
    gram = lax.dot_general(
        ydress_rows,
        lax.all_gather(ydress, "row", axis=0, tiled=True),
        contract,
        preferred_element_type=jnp.float32,
    )
    gap_rows = pair_gaps(
        occ_index, vir_index, eps_occ, eps_vir, row_position * rows_block, rows_block
    )
    gap_cols = pair_gaps(
        occ_index, vir_index, eps_occ, eps_vir, col_position * cols_block, cols_block
    )
    return (-gram / (gap_rows[:, None] + gap_cols[None, :])).astype(jnp.bfloat16)


def solution(mesh):
    return jax.shard_map(
        local,
        mesh=mesh,
        in_specs=(
            P(("grp", "row"), "col"),
            P("row", ("grp", "col")),
            P("grp"),
            P("grp"),
            P("grp"),
            P("grp"),
        ),
        out_specs=P(("grp", "row"), "col"),
        check_vma=False,
    )
```

profile of v0, /device:TPU:0, one launch (start us, length us, event | category | flops | bytes accessed | tf_op | source)
XLA Modules:
  0.0 794.7 jit_solution(10187947766805902085)
XLA Ops:
  6.5 0.0 all-gather.4.cloned.1.call-start
  6.5 4.1 copy.11
  10.6 0.0 all-gather.4.cloned.1.call-update
  10.6 0.0 reduce-scatter.2.cloned.1.call-start
  10.7 152.4 %all-gather.4.cloned.1.call-done = bf16[256,16384]{0,1:T(8,128)(2,1)} async-done(((bf16[256,4096]{0,1:T(8,128)(2,1)}), bf16[256,16384]{0,1:T(8,128)(2,1)}) %all-gather.4.cloned.1.call-update) | async-done | bytes 8388624 | tf_op jit(solution)/shard_map/all_gather | solution.py:25
  163.1 100.5 %all_to_all.38 = bf16[256,4,4096]{0,2,1:T(8,128)(2,1)} all-to-all(bf16[256,4,4096]{0,2,1:T(8,128)(2,1)} %bitcast.17), channel_id=1, replica_groups=mesh['grp'=2,'row'=4,'col'=4] {'row'}, dimensions={1} | all-to-all | bytes 16777216 | tf_op jit(solution)/shard_map/all_to_all | solution.py:26
  263.6 11.4 %copy.12 = bf16[4,256,4096]{2,1,0:T(8,128)(2,1)} copy(bf16[4,256,4096]{1,2,0:T(8,128)(2,1)} %bitcast.15) | data formatting | bytes 16777216 | tf_op jit(solution)/shard_map/all_to_all | solution.py:26
  275.1 43.0 %fusion.2 = f32[1024,4096]{1,0:T(8,128)} fusion(bf16[1024,4096]{1,0:T(8,128)(2,1)} %bitcast.18, bf16[4096,4096]{1,0:T(8,128)(2,1)} %param.6), kind=kOutput, calls=%fused_computation.13 | convolution fusion | flops 34359738368 | bytes 58720256 | tf_op jit(solution)/shard_map/dot_general | solution.py:28
  318.1 0.0 copy-start
  318.1 0.0 reduce-scatter.2.cloned.1.call-update
  318.1 0.0 all-gather.6.cloned.1.call-start
  318.2 122.4 %reduce-scatter.2.cloned.1.call-done = f32[256,4096]{1,0:T(8,128)} async-done(((f32[1024,4096]{1,0:T(8,128)}), f32[256,4096]{1,0:T(8,128)}) %reduce-scatter.2.cloned.1.call-update) | async-done | bytes 4194320 | tf_op jit(solution)/shard_map/reduce_scatter | solution.py:27
  440.6 0.0 copy-done
  440.6 4.1 add_convert_fusion
  444.7 0.0 all-gather.6.cloned.1.call-update
  444.7 0.0 all-gather.8.cloned.1.call-start
  444.8 0.5 all-gather.8.cloned.1.call-update
  445.3 149.2 %all-gather.6.cloned.1.call-done = bf16[256,16384]{1,0:T(8,128)(2,1)} async-done(((bf16[256,4096]{1,0:T(8,128)(2,1)}), bf16[256,16384]{1,0:T(8,128)(2,1)}) %all-gather.6.cloned.1.call-update) | async-done | bytes 8388624 | tf_op jit(solution)/shard_map/all_gather | solution.py:35
  594.5 8.6 %copy.16 = bf16[32,4,8,4096]{3,2,0,1:T(8,128)(2,1)} copy(bf16[32,4,8,4096]{3,2,1,0:T(8,128)(2,1)} %bitcast.16) | data formatting | bytes 16777216 | tf_op jit(solution)/shard_map/all_to_all | solution.py:36
  603.1 0.0 copy-start.1
  603.1 0.0 copy-start.2
  603.1 0.0 copy-start.4
  603.1 0.0 copy-start.3
  603.1 6.2 all-to-all-start.1
  609.3 0.0 copy-done.1
  609.3 0.0 copy-done.2
  609.3 0.0 copy-done.4
  609.3 0.2 select_reduce_fusion.3
  609.6 0.0 copy-done.3
  609.6 3.1 select_reduce_fusion.1
  612.8 78.0 %all-gather.8.cloned.1.call-done = bf16[1024,4096]{1,0:T(8,128)(2,1)} async-done(((bf16[256,4096]{1,0:T(8,128)(2,1)}), bf16[1024,4096]{1,0:T(8,128)(2,1)}) %all-gather.8.cloned.1.call-update) | async-done | bytes 8388624 | tf_op jit(solution)/shard_map/all_gather | solution.py:39
  690.8 49.8 %all-to-all-done.1 = bf16[256,4,4096]{2,0,1:T(8,128)(2,1)} async-done(((bf16[256,4,4096]{2,0,1:T(8,128)(2,1)}), bf16[256,4,4096]{2,0,1:T(8,128)(2,1)}, u32[]{:S(2)}, u32[]{:S(2)}) %all-to-all-start.1) | async-done | bytes 8388640 | tf_op jit(solution)/shard_map/all_to_all | solution.py:36
  740.6 47.6 %divide_convert_fusion = bf16[4096,4096]{1,0:T(8,128)(2,1)} fusion(bf16[1024,4096]{1,0:T(8,128)(2,1)} %bitcast.4, bf16[1024,4096]{1,0:T(8,128)(2,1)} %all-gather.8.cloned.1.call-done, f32[4096]{0:T(1024)S(1)} %sub.15, f32[4096]{0:T(1024)S(1)} %sub.14), kind=kOutput, calls=%fused_computation | convolution fusion | flops 34426847232 | bytes 50364416 | tf_op jit(solution)/shard_map/dot_general | solution.py:37
  (3 shorter events, 0.0 us)
Async XLA Ops:
  6.5 156.6 %all-gather.4.cloned.1.call-start = ((), (), s32[]{:S(2)}) async-start(), calls=%async_computation.3 | async-start | bytes 10485760 | tf_op jit(solution)/shard_map/all_gather | solution.py:25
  10.6 430.0 %reduce-scatter.2.cloned.1.call-start = ((), (), s32[]{:S(2)}) async-start(), calls=%async_computation.4 | async-start | bytes 20971520 | tf_op jit(solution)/shard_map/reduce_scatter | solution.py:27
  318.1 122.5 %copy-start = (bf16[256,4096]{1,0:T(8,128)(2,1)S(1)}, bf16[256,4096]{1,0:T(8,128)(2,1)}, u32[]{:S(2)}) copy-start(bf16[256,4096]{1,0:T(8,128)(2,1)} %param.7) | copy-start | bytes 6291460
  318.1 276.4 %all-gather.6.cloned.1.call-start = ((), (), s32[]{:S(2)}) async-start(), calls=%async_computation.5 | async-start | bytes 10485760 | tf_op jit(solution)/shard_map/all_gather | solution.py:35
  444.7 246.0 %all-gather.8.cloned.1.call-start = ((), (), s32[]{:S(2)}) async-start(), calls=%async_computation.6 | async-start | bytes 10485760 | tf_op jit(solution)/shard_map/all_gather | solution.py:39
  603.1 6.2 copy-start.1
  603.1 6.2 copy-start.2
  603.1 6.2 copy-start.4
  603.1 6.5 copy-start.3
  603.1 137.5 %all-to-all-start.1 = ((bf16[256,4,4096]{2,0,1:T(8,128)(2,1)}), bf16[256,4,4096]{2,0,1:T(8,128)(2,1)}, u32[]{:S(2)}, u32[]{:S(2)}) async-start(bf16[256,4,4096]{2,0,1:T(8,128)(2,1)} %bitcast.14), calls=%async_computation.2 | async-start | bytes 16777216 | tf_op jit(solution)/shard_map/all_to_all | solution.py:36
Sparse Core Ops, SparseCore 0:
  10.7 152.3 all-gather.3
  318.2 122.3 reduce-scatter.1
  444.9 149.5 all-gather.5
  595.9 94.8 all-gather.7
where the time goes:
time: 795 us
  waiting for transfers between devices  552 us (69%)
  blocking collectives  101 us (13%)
  matrix products  90.6 us (11%)
  local copies, waits for them, and re-layouts  24.1 us (3%)
  between operations  13.2 us (2%)
    all_gather x1, waiting for transfers between devices, local(): all_pairs = lax.all_gather(cholesky, 'col', axis=1, tiled=True)  152 us
    all_gather x1, waiting for transfers between devices, local(): ydress_pairs = lax.all_gather(ydress, 'col', axis=1, tiled=True)  149 us
    reduce_scatter x1, waiting for transfers between devices, local(): lax.psum_scatter(jnp.dot(chol_rows, amplitudes, preferred_element_type=jn...  122 us
    all_to_all x1, blocking collectives, local(): lax.all_to_all(all_pairs, 'row', split_axis=1, concat_axis=0, tiled=True)  101 us
    all_gather x1, waiting for transfers between devices, local(): lax.all_gather(ydress, 'row', axis=0, tiled=True)  78 us
    all_to_all x1, waiting for transfers between devices, local(): lax.all_to_all(ydress_pairs, 'row', split_axis=1, concat_axis=0, tiled=True)  49.8 us
    dot_general x1, matrix products, local(): lax.dot_general(ydress_rows, lax.all_gather(ydress, 'row', axis=0, tiled=...  47.6 us
    dot_general x1, matrix products, local(): jnp.dot(chol_rows, amplitudes, preferred_element_type=jnp.float32)  43 us
  transfers between devices with their start and end apart: 5, of which 5 were waited for; matrix products, arithmetic and copies ran while one was open for 2% of the time, Pallas kernels for 0%

commit v1 on v0

v1 whole, which is shorter than its diff:
```python
import functools

import jax
import jax.numpy as jnp
from jax import lax
from jax.experimental import pallas as pl
from jax.experimental.pallas import tpu as pltpu
from jax.sharding import PartitionSpec as P

MESH = pl.DeviceIdType.MESH


def pair_gaps(occ_index, vir_index, eps_occ, eps_vir, begin_pair, pair_count):
    occ_rows = lax.dynamic_slice_in_dim(occ_index, begin_pair, pair_count, 0)
    vir_rows = lax.dynamic_slice_in_dim(vir_index, begin_pair, pair_count, 0)
    occ_table = jnp.arange(eps_occ.shape[0], dtype=jnp.int32)
    vir_table = jnp.arange(eps_vir.shape[0], dtype=jnp.int32)
    occ_energy = jnp.sum(
        jnp.where(occ_rows[:, None] == occ_table[None, :], eps_occ[None, :], 0.0), axis=1
    )
    vir_energy = jnp.sum(
        jnp.where(vir_rows[:, None] == vir_table[None, :], eps_vir[None, :], 0.0), axis=1
    )
    return vir_energy - occ_energy


def enter(row_count, col_count, me_row, me_col):
    barrier = pltpu.get_barrier_semaphore()
    for step in range(1, row_count):
        pl.semaphore_signal(
            barrier,
            inc=1,
            device_id={"row": lax.rem(me_row + step, row_count)},
            device_id_type=MESH,
        )
    for condition, where in ((me_col > 0, -1), (me_col < col_count - 1, 1)):

        @pl.when(condition)
        def _():
            pl.semaphore_signal(
                barrier, inc=1, device_id={"col": me_col + where}, device_id_type=MESH
            )

    neighbours = jnp.minimum(me_col, 1) + jnp.minimum(col_count - 1 - me_col, 1)
    pl.semaphore_wait(barrier, row_count - 1 + neighbours)


class Gather:
    def __init__(self, row_count, col_count, pieces, own, rows, held, sems):
        self.row_count, self.col_count, self.pieces = row_count, col_count, pieces
        self.own, self.rows, self.held = own, rows, held
        (self.load, self.send_line, self.recv_line, self.send_row, self.recv_row, self.keep) = sems
        self.me_row, self.me_col = lax.axis_index("row"), lax.axis_index("col")
        self.depth = own.shape[0] // pieces
        self.share = row_count // col_count
        self.width = own.shape[1] // self.share

    def part(self, piece):
        return pl.ds(piece * self.depth, self.depth)

    def load_copy(self, piece):
        return pltpu.make_async_copy(
            self.own.at[self.part(piece), :],
            self.held.at[self.me_col, self.part(piece), :],
            self.load.at[piece],
        )

    def line_copy(self, side, block, hops, piece):
        ref = self.held.at[block, self.part(piece), :]
        return pltpu.make_async_remote_copy(
            src_ref=ref,
            dst_ref=ref,
            send_sem=self.send_line.at[side, hops, piece],
            recv_sem=self.recv_line.at[side, hops, piece],
            device_id={"col": self.me_col + (1 if side == 0 else -1)},
            device_id_type=MESH,
        )

    def row_copy(self, block, index, piece):
        return pltpu.make_async_remote_copy(
            src_ref=self.held.at[
                block, self.part(piece), pl.ds(index * self.width, self.width)
            ],
            dst_ref=self.rows.at[self.me_row, self.part(piece), :],
            send_sem=self.send_row.at[block, index, piece],
            recv_sem=self.recv_row.at[self.me_row, piece],
            device_id={"row": block * self.share + index},
            device_id_type=MESH,
        )

    def keep_copy(self, block, index, piece):
        return pltpu.make_async_copy(
            self.held.at[block, self.part(piece), pl.ds(index * self.width, self.width)],
            self.rows.at[self.me_row, self.part(piece), :],
            self.keep.at[piece],
        )

    def on(self, side):
        return self.me_col < self.col_count - 1 if side == 0 else self.me_col > 0

    def spread(self, block, piece):
        for index in range(self.share):
            target = block * self.share + index

            @pl.when(target == self.me_row)
            def _():
                self.keep_copy(block, index, piece).start()

            @pl.when(target != self.me_row)
            def _():
                self.row_copy(block, index, piece).start()

    def begin(self, piece):
        self.load_copy(piece).wait()
        for side in range(2):

            @pl.when(self.on(side))
            def _():
                self.line_copy(side, self.me_col, 0, piece).start()

        self.spread(self.me_col, piece)

    def source(self, side, hops):
        block = self.me_col - hops if side == 0 else self.me_col + hops
        exists = self.me_col >= hops if side == 0 else self.me_col + hops < self.col_count
        return block, exists

    def arrive(self, hops, piece):
        for side in range(2):
            block, exists = self.source(side, hops)

            @pl.when(exists)
            def _():
                self.line_copy(side, block, hops - 1, piece).wait_recv()

                if hops < self.col_count - 1:

                    @pl.when(self.on(side))
                    def _():
                        self.line_copy(side, block, hops, piece).start()

                self.spread(block, piece)

    def wait_rows(self, piece):
        for other in range(self.row_count):

            @pl.when(other != self.me_row)
            def _():
                pltpu.make_async_remote_copy(
                    src_ref=self.rows.at[other, self.part(piece), :],
                    dst_ref=self.rows.at[other, self.part(piece), :],
                    send_sem=self.send_row.at[0, 0, piece],
                    recv_sem=self.recv_row.at[other, piece],
                    device_id={"row": other},
                    device_id_type=MESH,
                ).wait_recv()

        for block in range(self.col_count):
            for index in range(self.share):

                @pl.when(block * self.share + index == self.me_row)
                def _():
                    self.keep_copy(block, index, piece).wait()

    def wait_sends(self, piece):
        for side in range(2):
            for hops in range(self.col_count - 1):
                block, exists = self.source(side, hops)

                @pl.when(jnp.logical_and(exists, self.on(side)))
                def _():
                    self.line_copy(side, block, hops, piece).wait_send()

        for block in range(self.col_count):
            for index in range(self.share):

                @pl.when(block * self.share + index != self.me_row)
                def _():
                    self.row_copy(block, index, piece).wait_send()


def gather_sems(row_count, col_count, pieces):
    return [
        pltpu.SemaphoreType.DMA((pieces,)),
        pltpu.SemaphoreType.DMA((2, col_count, pieces)),
        pltpu.SemaphoreType.DMA((2, col_count, pieces)),
        pltpu.SemaphoreType.DMA((col_count, row_count // col_count, pieces)),
        pltpu.SemaphoreType.DMA((row_count, pieces)),
        pltpu.SemaphoreType.DMA((pieces,)),
    ]


class Columns:
    def __init__(self, row_count, pieces, own, cols, sems):
        self.row_count, self.pieces, self.own, self.cols = row_count, pieces, own, cols
        self.load, self.send, self.recv, self.send_on = sems
        self.me_row = lax.axis_index("row")
        self.partner = self.me_row + 1 - 2 * lax.rem(self.me_row, 2)
        self.depth = own.shape[0] // pieces

    def part(self, piece):
        return pl.ds(piece * self.depth, self.depth)

    def copy(self, owner, target, sem, piece, src=None):
        dst = self.cols.at[owner, self.part(piece), :]
        return pltpu.make_async_remote_copy(
            src_ref=dst if src is None else src,
            dst_ref=dst,
            send_sem=sem,
            recv_sem=self.recv.at[owner, piece],
            device_id={"row": target},
            device_id_type=MESH,
        )

    def peers(self):
        peers = [(0, self.partner)]
        for step in range(1, self.row_count // 2):
            peers.append((step, lax.rem(self.me_row + 2 * step, self.row_count)))
        return peers

    def first(self, slot, target, piece, src):
        return self.copy(self.me_row, target, self.send.at[slot, piece], piece, src)

    def begin(self, piece, src):
        for slot, target in self.peers():
            self.first(slot, target, piece, src).start()

    def arrive(self, piece):
        for slot, owner in self.peers()[1:]:
            self.copy(owner, self.partner, self.send_on.at[slot, piece], piece).wait_recv()
            self.copy(owner, self.partner, self.send_on.at[slot, piece], piece).start()

    def finish(self, piece, src):
        for slot, target in self.peers():
            self.first(slot, target, piece, src).wait_send()
        self.copy(self.partner, self.partner, self.send.at[0, piece], piece).wait_recv()
        for slot, owner in self.peers()[1:]:
            self.copy(owner, self.partner, self.send_on.at[slot, piece], piece).wait_send()
            theirs = lax.rem(self.partner + 2 * slot, self.row_count)
            self.copy(theirs, self.partner, self.send.at[0, piece], piece).wait_recv()


def columns_sems(row_count, pieces):
    return [
        pltpu.SemaphoreType.DMA((pieces,)),
        pltpu.SemaphoreType.DMA((row_count // 2, pieces)),
        pltpu.SemaphoreType.DMA((row_count, pieces)),
        pltpu.SemaphoreType.DMA((row_count // 2, pieces)),
    ]


def gather_kernel(row_count, col_count, pieces, with_cols, *refs):
    own, rows = refs[0], refs[1]
    rest = refs[2:]
    columns = None
    if with_cols:
        cols, held = rest[0], rest[1]
        sems, cols_sems = rest[2:8], rest[8:12]
        columns = Columns(row_count, pieces, own, cols, cols_sems)
    else:
        held, sems = rest[0], rest[1:7]
    gather = Gather(row_count, col_count, pieces, own, rows, held, sems)
    for piece in range(pieces):
        gather.load_copy(piece).start()
    enter(row_count, col_count, gather.me_row, gather.me_col)

    def source(piece):
        return held.at[gather.me_col, gather.part(piece), :]

    def own_cols(piece):
        return pltpu.make_async_copy(
            source(piece), cols.at[gather.me_row, gather.part(piece), :], columns.load.at[piece]
        )

    def begin(piece):
        gather.begin(piece)
        if with_cols:
            own_cols(piece).start()
            columns.begin(piece, source(piece))

    for piece in range(min(2, pieces)):
        begin(piece)
    for step in range(pieces + col_count - 2):
        if step + 2 < pieces:
            begin(step + 2)
        for hops in range(1, col_count):
            if 0 <= step - hops + 1 < pieces:
                gather.arrive(hops, step - hops + 1)
        if with_cols and step < pieces:
            columns.arrive(step)
    for piece in range(pieces):
        gather.wait_rows(piece)
        gather.wait_sends(piece)
        if with_cols:
            own_cols(piece).wait()
            columns.finish(piece, source(piece))


def gather_pairs(own, row_count, col_count, with_cols, collective_id):
    depth, width = own.shape
    pieces = max(1, min(4, depth // 16))
    rows = jax.ShapeDtypeStruct(
        (row_count, depth, width * col_count // row_count), own.dtype
    )
    cols = jax.ShapeDtypeStruct((row_count, depth, width), own.dtype)
    out_shape = (rows, cols) if with_cols else (rows,)
    scratch = [pltpu.VMEM((col_count, depth, width), own.dtype)]
    scratch += gather_sems(row_count, col_count, pieces)
    if with_cols:
        scratch += columns_sems(row_count, pieces)
    out = pl.pallas_call(
        functools.partial(gather_kernel, row_count, col_count, pieces, with_cols),
        out_shape=out_shape,
        in_specs=[pl.BlockSpec(memory_space=pl.ANY)],
        out_specs=tuple(pl.BlockSpec(memory_space=pl.ANY) for _ in out_shape),
        scratch_shapes=scratch,
        compiler_params=pltpu.CompilerParams(
            collective_id=collective_id, has_side_effects=True
        ),
        name="gather_cols" if with_cols else "gather_rows",
    )(own)
    return [item.reshape(row_count * depth, item.shape[2]) for item in out]


def local(row_count, col_count, amplitudes, cholesky, occ_index, vir_index, eps_occ, eps_vir):
    row_position = lax.axis_index("row")
    col_position = lax.axis_index("col")
    rows_block, cols_block = amplitudes.shape
    (chol_rows,) = gather_pairs(cholesky, row_count, col_count, False, 0)
    dressed = lax.psum_scatter(
        jnp.dot(chol_rows, amplitudes, preferred_element_type=jnp.float32),
        "row",
        scatter_dimension=0,
        tiled=True,
    )
    ydress = (cholesky.astype(jnp.float32) + dressed).astype(jnp.bfloat16)
    contract = (((0,), (0,)), ((), ()))
    ydress_rows, ydress_cols = gather_pairs(ydress, row_count, col_count, True, 1)
    gram = lax.dot_general(
        ydress_rows, ydress_cols, contract, preferred_element_type=jnp.float32
    )
    gap_rows = pair_gaps(
        occ_index, vir_index, eps_occ, eps_vir, row_position * rows_block, rows_block
    )
    gap_cols = pair_gaps(
        occ_index, vir_index, eps_occ, eps_vir, col_position * cols_block, cols_block
    )
    return (-gram / (gap_rows[:, None] + gap_cols[None, :])).astype(jnp.bfloat16)


def solution(mesh):
    return jax.shard_map(
        functools.partial(local, mesh.shape["row"], mesh.shape["col"]),
        mesh=mesh,
        in_specs=(
            P(("grp", "row"), "col"),
            P("row", ("grp", "col")),
            P("grp"),
            P("grp"),
            P("grp"),
            P("grp"),
        ),
        out_specs=P(("grp", "row"), "col"),
        check_vma=False,
    )
```

time: 795 us -> 536 us (0.67)
  waiting for transfers between devices: 552 us -> 121 us
  Pallas kernels: 0 us -> 302 us
  blocking collectives: 101 us -> 0 us
  local copies, waits for them, and re-layouts: 24.1 us -> 0.83 us
    all_gather x3 -> x0, waiting for transfers between devices: 380 us -> none  [the longest x1 152 us: local(): all_pairs = lax.all_gather(cholesky, 'col', axis=1, tiled=True)]
    pallas_call x0 -> x2, Pallas kernels: none -> 302 us  [gather_pairs(): pl.pallas_call(functools.partial(gather_kernel, row_count, col_count, pie...]
    all_to_all x1 -> x0, blocking collectives: 101 us -> none  [local(): lax.all_to_all(all_pairs, 'row', split_axis=1, concat_axis=0, tiled=True)]
    all_to_all x1 -> x0, waiting for transfers between devices: 49.8 us -> none  [local(): lax.all_to_all(ydress_pairs, 'row', split_axis=1, concat_axis=0, tiled=True)]
    all_to_all x2 -> x0, local copies, waits for them, and re-layouts: 20 us -> none  [the longest x1 11.4 us: local(): lax.all_to_all(all_pairs, 'row', split_axis=1, concat_axis=0, tiled=True)]
  transfers between devices with their start and end apart: 5 -> 1, of which waited for: 5 -> 1; matrix products, arithmetic and copies ran while one was open for 2% -> 1% of each run, Pallas kernels for 0% -> 0%
where the time goes in v1:
time: 536 us
  Pallas kernels  302 us (56%)
  waiting for transfers between devices  121 us (23%)
  matrix products  90.7 us (17%)
  between operations  13.5 us (3%)
  other arithmetic  7.45 us (1%)
    pallas_call x2, Pallas kernels, gather_pairs(): pl.pallas_call(functools.partial(gather_kernel, row_count, col_count, pie...  302 us
    reduce_scatter x1, waiting for transfers between devices, local(): lax.psum_scatter(jnp.dot(chol_rows, amplitudes, preferred_element_type=jn...  121 us
    dot_general x1, matrix products, local(): lax.dot_general(ydress_rows, ydress_cols, contract, preferred_element_typ...  47.6 us
    dot_general x1, matrix products, local(): jnp.dot(chol_rows, amplitudes, preferred_element_type=jnp.float32)  43 us
  transfers between devices with their start and end apart: 1, of which 1 were waited for; matrix products, arithmetic and copies ran while one was open for 1% of the time, Pallas kernels for 0%

profile of v1, /device:TPU:0, one launch (start us, length us, event | category | flops | bytes accessed | tf_op | source)
XLA Modules:
  0.0 536.0 jit_solution(2289297314991201978)
XLA Ops:
  6.5 0.0 reduce-scatter.2.cloned.1.call-start
  6.5 152.3 %gather_rows.1 = bf16[4,256,4096]{2,1,0:T(8,128)(2,1)} custom-call(bf16[256,4096]{1,0:T(8,128)(2,1)} %refs_0_.1), custom_call_target="tpu_custom_call" | custom-call | tf_op jit(solution)/shard_map/gather_rows/pallas_call | solution.py:311
  158.9 43.0 %fusion.4 = f32[1024,4096]{1,0:T(8,128)} fusion(bf16[1024,4096]{1,0:T(8,128)(2,1)} %bitcast.11, bf16[4096,4096]{1,0:T(8,128)(2,1)} %param.6), kind=kOutput, calls=%fused_computation.14 | convolution fusion | flops 34359738368 | bytes 58720256 | tf_op jit(solution)/shard_map/dot_general | solution.py:331
  201.9 0.0 copy-start.1
  201.9 0.0 copy-start.2
  201.9 0.0 copy-start.4
  201.9 0.0 copy-start.3
  202.0 0.0 copy-start
  202.0 0.0 reduce-scatter.2.cloned.1.call-update
  202.0 0.8 copy-done.1
  202.8 0.0 copy-done.2
  202.8 0.0 copy-done.4
  202.8 0.2 select_reduce_fusion.3
  203.1 0.0 copy-done.3
  203.1 3.1 select_reduce_fusion.1
  206.2 121.4 %reduce-scatter.2.cloned.1.call-done = f32[256,4096]{1,0:T(8,128)} async-done(((f32[1024,4096]{1,0:T(8,128)}), f32[256,4096]{1,0:T(8,128)}) %reduce-scatter.2.cloned.1.call-update) | async-done | bytes 4194320 | tf_op jit(solution)/shard_map/reduce_scatter | solution.py:330
  327.6 0.0 copy-done
  327.6 4.1 add_convert_fusion.refs_0_
  331.7 149.8 %gather_cols.1 = (bf16[4,256,4096]{2,1,0:T(8,128)(2,1)}, bf16[4,256,4096]{2,1,0:T(8,128)(2,1)}) custom-call(bf16[256,4096]{1,0:T(8,128)(2,1)} %add_convert_fusion.refs_0_), custom_call_target="tpu_custom_call" | custom-call | tf_op jit(solution)/shard_map/gather_cols/pallas_call | solution.py:311
  481.5 47.6 %fusion.1 = bf16[4096,4096]{1,0:T(8,128)(2,1)} fusion(bf16[4,256,4096]{2,1,0:T(8,128)(2,1)} %get-tuple-element.7, bf16[4,256,4096]{2,1,0:T(8,128)(2,1)} %get-tuple-element.8, f32[4096]{0:T(1024)S(1)} %sub.15, f32[4096]{0:T(1024)S(1)} %sub.14), kind=kOutput, calls=%fused_computation.2 | convolution fusion | flops 34426847232 | bytes 50364416 | tf_op jit(solution)/shard_map/dot_general | solution.py:339
  (3 shorter events, 0.0 us)
Async XLA Ops:
  6.5 321.1 %reduce-scatter.2.cloned.1.call-start = ((), (), s32[]{:S(2)}) async-start(), calls=%async_computation.1 | async-start | bytes 20971520 | tf_op jit(solution)/shard_map/reduce_scatter | solution.py:330
  201.9 0.8 copy-start.1
  201.9 0.9 copy-start.2
  201.9 0.9 copy-start.4
  201.9 1.1 copy-start.3
  202.0 125.7 %copy-start = (bf16[256,4096]{1,0:T(8,128)(2,1)S(1)}, bf16[256,4096]{1,0:T(8,128)(2,1)}, u32[]{:S(2)}) copy-start(bf16[256,4096]{1,0:T(8,128)(2,1)} %refs_0_.1) | copy-start | bytes 6291460
Sparse Core Ops, SparseCore 0:
  202.1 125.4 reduce-scatter.1

commit v2 on v1

--- a/solution.py
+++ b/solution.py
@@ -46,7 +46,8 @@
 
 
 class Gather:
-    def __init__(self, row_count, col_count, pieces, own, rows, held, sems):
+    def __init__(self, row_count, col_count, pieces, own, rows, held, sems, direct=False):
+        self.direct = direct
         self.row_count, self.col_count, self.pieces = row_count, col_count, pieces
         self.own, self.rows, self.held = own, rows, held
         (self.load, self.send_line, self.recv_line, self.send_row, self.recv_row, self.keep) = sems
@@ -65,60 +66,79 @@
             self.load.at[piece],
         )
 
+    def block_ref(self, block, piece, mine):
+        if mine and self.direct:
+            return self.own.at[self.part(piece), :]
+        return self.held.at[block, self.part(piece), :]
+
+    def block_part(self, block, index, piece, mine):
+        columns = pl.ds(index * self.width, self.width)
+        if mine and self.direct:
+            return self.own.at[self.part(piece), columns]
+        return self.held.at[block, self.part(piece), columns]
+
+    def row_ref(self, owner, target, piece):
+        if not self.direct:
+            return self.rows.at[owner, self.part(piece), :]
+        half = self.row_count // 2
+        other = lax.rem(owner + target, 2)
+        base = target + other * (1 - 2 * lax.rem(target, 2))
+        slot = lax.rem(owner - base + self.row_count, self.row_count) // 2 + other * half
+        begin = pl.multiple_of(slot * self.depth, self.depth)
+        return self.rows.at[piece, pl.ds(begin, self.depth), :]
+
     def line_copy(self, side, block, hops, piece):
-        ref = self.held.at[block, self.part(piece), :]
         return pltpu.make_async_remote_copy(
-            src_ref=ref,
-            dst_ref=ref,
+            src_ref=self.block_ref(block, piece, hops == 0),
+            dst_ref=self.held.at[block, self.part(piece), :],
             send_sem=self.send_line.at[side, hops, piece],
             recv_sem=self.recv_line.at[side, hops, piece],
             device_id={"col": self.me_col + (1 if side == 0 else -1)},
             device_id_type=MESH,
         )
 
-    def row_copy(self, block, index, piece):
+    def row_copy(self, block, index, piece, mine=False):
         return pltpu.make_async_remote_copy(
-            src_ref=self.held.at[
-                block, self.part(piece), pl.ds(index * self.width, self.width)
-            ],
-            dst_ref=self.rows.at[self.me_row, self.part(piece), :],
+            src_ref=self.block_part(block, index, piece, mine),
+            dst_ref=self.row_ref(self.me_row, block * self.share + index, piece),
             send_sem=self.send_row.at[block, index, piece],
             recv_sem=self.recv_row.at[self.me_row, piece],
             device_id={"row": block * self.share + index},
             device_id_type=MESH,
         )
 
-    def keep_copy(self, block, index, piece):
+    def keep_copy(self, block, index, piece, mine=False):
         return pltpu.make_async_copy(
-            self.held.at[block, self.part(piece), pl.ds(index * self.width, self.width)],
-            self.rows.at[self.me_row, self.part(piece), :],
+            self.block_part(block, index, piece, mine),
+            self.row_ref(self.me_row, self.me_row, piece),
             self.keep.at[piece],
         )
 
     def on(self, side):
         return self.me_col < self.col_count - 1 if side == 0 else self.me_col > 0
 
-    def spread(self, block, piece):
+    def spread(self, block, piece, mine=False):
         for index in range(self.share):
             target = block * self.share + index
 
             @pl.when(target == self.me_row)
             def _():
-                self.keep_copy(block, index, piece).start()
+                self.keep_copy(block, index, piece, mine).start()
 
             @pl.when(target != self.me_row)
             def _():
-                self.row_copy(block, index, piece).start()
+                self.row_copy(block, index, piece, mine).start()
 
     def begin(self, piece):
-        self.load_copy(piece).wait()
+        if not self.direct:
+            self.load_copy(piece).wait()
         for side in range(2):
 
             @pl.when(self.on(side))
             def _():
                 self.line_copy(side, self.me_col, 0, piece).start()
 
-        self.spread(self.me_col, piece)
+        self.spread(self.me_col, piece, True)
 
     def source(self, side, hops):
         block = self.me_col - hops if side == 0 else self.me_col + hops
@@ -147,8 +167,8 @@
             @pl.when(other != self.me_row)
             def _():
                 pltpu.make_async_remote_copy(
-                    src_ref=self.rows.at[other, self.part(piece), :],
-                    dst_ref=self.rows.at[other, self.part(piece), :],
+                    src_ref=self.row_ref(other, self.me_row, piece),
+                    dst_ref=self.row_ref(other, self.me_row, piece),
                     send_sem=self.send_row.at[0, 0, piece],
                     recv_sem=self.recv_row.at[other, piece],
                     device_id={"row": other},
@@ -322,18 +342,178 @@
     return [item.reshape(row_count * depth, item.shape[2]) for item in out]
 
 
+def dress_kernel(
+    row_count, col_count, pieces, amplitudes, own, held, dressed, table, rows, mine, kept,
+    to_partner, from_partner, to_peer, from_peer, chol, table_sem, chol_sem,
+    partner_send, partner_recv, peer_send, peer_recv, *sems
+):
+    gather = Gather(row_count, col_count, pieces, own, rows, held, sems, direct=True)
+    me_row, depth = gather.me_row, gather.depth
+    partner = me_row + 1 - 2 * lax.rem(me_row, 2)
+    half = row_count // 2
+    split = table_sem.shape[0]
+    chunk = table.shape[0] // split
+    tile = min(512, table.shape[1])
+    tiles = table.shape[1] // tile
+
+    def table_copy(index):
+        span = pl.ds(index * chunk, chunk)
+        return pltpu.make_async_copy(
+            amplitudes.at[span, :], table.at[span, :], table_sem.at[index]
+        )
+
+    def chol_copy(piece):
+        return pltpu.make_async_copy(
+            own.at[gather.part(piece), :], chol.at[piece], chol_sem.at[piece]
+        )
+
+    def partner_copy(piece):
+        return pltpu.make_async_remote_copy(
+            src_ref=to_partner.at[piece % 2],
+            dst_ref=from_partner.at[piece],
+            send_sem=partner_send.at[piece],
+            recv_sem=partner_recv.at[piece],
+            device_id={"row": partner},
+            device_id_type=MESH,
+        )
+
+    def peer_copy(step, piece):
+        return pltpu.make_async_remote_copy(
+            src_ref=to_peer.at[piece % 2, step - 1],
+            dst_ref=from_peer.at[piece, half - step - 1],
+            send_sem=peer_send.at[piece, step],
+            recv_sem=peer_recv.at[piece, half - step],
+            device_id={"row": lax.rem(me_row + 2 * step, row_count)},
+            device_id_type=MESH,
+        )
+
+    def multiply(piece):
+        if piece >= 2:
+            partner_copy(piece - 2).wait_send()
+
+        @pl.loop(0, tiles)
+        def _(index):
+            span = pl.ds(pl.multiple_of(index * tile, tile), tile)
+            product = jnp.dot(
+                rows[piece], table[:, span], preferred_element_type=jnp.float32
+            )
+            mine[:, span] = product[: half * depth]
+            to_partner[piece % 2, :, span] = product[half * depth :].astype(jnp.bfloat16)
+
+        partner_copy(piece).start()
+
+    def pair(piece):
+        partner_copy(piece).wait_recv()
+        if piece >= 2:
+            for step in range(1, half):
+                peer_copy(step, piece - 2).wait_send()
+
+        @pl.loop(0, tiles)
+        def _(index):
+            span = pl.ds(pl.multiple_of(index * tile, tile), tile)
+            both = mine[:, span] + from_partner[piece, :, span].astype(jnp.float32)
+            kept[piece % 2, :, span] = both[:depth]
+            for step in range(1, half):
+                to_peer[piece % 2, step - 1, :, span] = both[
+                    step * depth : (step + 1) * depth
+                ].astype(jnp.bfloat16)
+
+        for step in range(1, half):
+            peer_copy(step, piece).start()
+
+    def close(piece):
+        chol_copy(piece).wait()
+        for step in range(1, half):
+            peer_copy(step, piece).wait_recv()
+
+        @pl.loop(0, tiles)
+        def _(index):
+            span = pl.ds(pl.multiple_of(index * tile, tile), tile)
+            total = kept[piece % 2, :, span]
+            for step in range(1, half):
+                total = total + from_peer[piece, step - 1, :, span].astype(jnp.float32)
+            total = chol[piece, :, span].astype(jnp.float32) + total
+            dressed[gather.part(piece), span] = total.astype(jnp.bfloat16)
+
+    enter(row_count, col_count, gather.me_row, gather.me_col)
+    for piece in range(min(2, pieces)):
+        gather.begin(piece)
+    for index in range(split):
+        table_copy(index).start()
+    for piece in range(pieces):
+        chol_copy(piece).start()
+    for step in range(pieces + col_count):
+        if step + 2 < pieces:
+            gather.begin(step + 2)
+        for hops in range(1, col_count):
+            if 0 <= step - hops + 1 < pieces:
+                gather.arrive(hops, step - hops + 1)
+        piece = step - (col_count - 2)
+        if 0 <= piece - 1 < pieces:
+            pair(piece - 1)
+        if 0 <= piece - 2 < pieces:
+            close(piece - 2)
+        if 0 <= piece < pieces:
+            gather.wait_rows(piece)
+            if piece == 0:
+                for index in range(split):
+                    table_copy(index).wait()
+            multiply(piece)
+    for piece in range(pieces):
+        gather.wait_sends(piece)
+        if piece >= pieces - 2:
+            partner_copy(piece).wait_send()
+            for step in range(1, half):
+                peer_copy(step, piece).wait_send()
+
+
+def dress_pairs(amplitudes, own, row_count, col_count, collective_id):
+    depth, width = own.shape
+    pieces = max(1, min(4, depth // 16))
+    depth_piece, half = depth // pieces, row_count // 2
+    bf16, f32, dma = jnp.bfloat16, jnp.float32, pltpu.SemaphoreType.DMA
+    scratch = [
+        pltpu.VMEM(amplitudes.shape, bf16),
+        pltpu.VMEM((pieces, row_count * depth_piece, amplitudes.shape[0]), bf16),
+        pltpu.VMEM((half * depth_piece, width), f32),
+        pltpu.VMEM((2, depth_piece, width), f32),
+        pltpu.VMEM((2, half * depth_piece, width), bf16),
+        pltpu.VMEM((pieces, half * depth_piece, width), bf16),
+        pltpu.VMEM((2, half - 1, depth_piece, width), bf16),
+        pltpu.VMEM((pieces, half - 1, depth_piece, width), bf16),
+        pltpu.VMEM((pieces, depth_piece, width), bf16),
+        dma((4,)),
+        dma((pieces,)),
+        dma((pieces,)),
+        dma((pieces,)),
+        dma((pieces, half)),
+        dma((pieces, half)),
+    ] + gather_sems(row_count, col_count, pieces)
+    _, dressed = pl.pallas_call(
+        functools.partial(dress_kernel, row_count, col_count, pieces),
+        out_shape=(
+            jax.ShapeDtypeStruct((col_count, depth, width), bf16),
+            jax.ShapeDtypeStruct((depth, width), bf16),
+        ),
+        in_specs=[pl.BlockSpec(memory_space=pl.ANY)] * 2,
+        out_specs=(
+            pl.BlockSpec(memory_space=pl.ANY),
+            pl.BlockSpec(memory_space=pltpu.VMEM),
+        ),
+        scratch_shapes=scratch,
+        compiler_params=pltpu.CompilerParams(
+            collective_id=collective_id, has_side_effects=True, vmem_limit_bytes=67043328
+        ),
+        name="dress",
+    )(amplitudes, own)
+    return dressed
+
+
 def local(row_count, col_count, amplitudes, cholesky, occ_index, vir_index, eps_occ, eps_vir):
     row_position = lax.axis_index("row")
     col_position = lax.axis_index("col")
     rows_block, cols_block = amplitudes.shape
-    (chol_rows,) = gather_pairs(cholesky, row_count, col_count, False, 0)
-    dressed = lax.psum_scatter(
-        jnp.dot(chol_rows, amplitudes, preferred_element_type=jnp.float32),
-        "row",
-        scatter_dimension=0,
-        tiled=True,
-    )
-    ydress = (cholesky.astype(jnp.float32) + dressed).astype(jnp.bfloat16)
+    ydress = dress_pairs(amplitudes, cholesky, row_count, col_count, 0)
     contract = (((0,), (0,)), ((), ()))
     ydress_rows, ydress_cols = gather_pairs(ydress, row_count, col_count, True, 1)
     gram = lax.dot_general(

time: 536 us -> 408 us (0.76)
  waiting for transfers between devices: 121 us -> 0 us
  Pallas kernels: 302 us -> 350 us
  matrix products: 90.7 us -> 48 us
  between operations: 13.5 us -> 0.03 us
    pallas_call x0 -> x1, Pallas kernels: none -> 204 us  [dress_pairs(): pl.pallas_call(functools.partial(dress_kernel, row_count, col_count, piec...]
    pallas_call x2 -> x1, Pallas kernels: 302 us -> 146 us  [gather_pairs(): pl.pallas_call(functools.partial(gather_kernel, row_count, col_count, pie...]
    reduce_scatter x1 -> x0, waiting for transfers between devices: 121 us -> none  [local(): lax.psum_scatter(jnp.dot(chol_rows, amplitudes, preferred_element_type=jn...]
    dot_general x1 -> x0, matrix products: 43 us -> none  [local(): jnp.dot(chol_rows, amplitudes, preferred_element_type=jnp.float32)]
  transfers between devices with their start and end apart: 1 -> 0, of which waited for: 1 -> 0; matrix products, arithmetic and copies ran while one was open for 1% -> 0% of each run, Pallas kernels for 0% -> 0%
where the time goes in v2:
time: 408 us; the launch traced here: 405 us
  Pallas kernels  350 us (86%)
  matrix products  48 us (12%)
  other arithmetic  5.91 us (1%)
    pallas_call x1, Pallas kernels, dress_pairs(): pl.pallas_call(functools.partial(dress_kernel, row_count, col_count, piec...  204 us
    pallas_call x1, Pallas kernels, gather_pairs(): pl.pallas_call(functools.partial(gather_kernel, row_count, col_count, pie...  146 us
    dot_general x1, matrix products, local(): lax.dot_general(ydress_rows, ydress_cols, contract, preferred_element_typ...  48 us

profile of v2, /device:TPU:0, one launch (start us, length us, event | category | flops | bytes accessed | tf_op | source)
XLA Modules:
  0.0 405.1 jit_solution(14166795348379825076)
XLA Ops:
  0.0 0.8 fusion.2
  0.8 0.9 select_reduce_fusion.3
  1.7 3.8 select_reduce_fusion.1
  5.5 0.6 sub.14
  6.1 0.6 sub.15
  6.7 203.9 %dress.1 = (bf16[4,256,4096]{2,1,0:T(8,128)(2,1)}, bf16[256,4096]{1,0:T(8,128)(2,1)}) custom-call(bf16[4096,4096]{1,0:T(8,128)(2,1)} %amplitudes.1, bf16[256,4096]{1,0:T(8,128)(2,1)} %own.1), custom_call_target="tpu_custom_call" | custom-call | tf_op jit(solution)/shard_map/dress/pallas_call | solution.py:492
  210.6 146.4 %gather_cols.1 = (bf16[4,256,4096]{2,1,0:T(8,128)(2,1)}, bf16[4,256,4096]{2,1,0:T(8,128)(2,1)}) custom-call(bf16[256,4096]{1,0:T(8,128)(2,1)} %get-tuple-element.8.refs_0_), custom_call_target="tpu_custom_call" | custom-call | tf_op jit(solution)/shard_map/gather_cols/pallas_call | solution.py:331
  357.0 48.0 %fusion.1 = bf16[4096,4096]{1,0:T(8,128)(2,1)} fusion(bf16[4,256,4096]{2,1,0:T(8,128)(2,1)} %get-tuple-element.9, bf16[4,256,4096]{2,1,0:T(8,128)(2,1)} %get-tuple-element.10, f32[4096]{0:T(1024)} %sub.15, f32[4096]{0:T(1024)} %sub.14), kind=kOutput, calls=%fused_computation.2 | convolution fusion | flops 34426847232 | bytes 50364416 | tf_op jit(solution)/shard_map/dot_general | solution.py:519

commit v3 on v2

--- a/solution.py
+++ b/solution.py
@@ -46,11 +46,11 @@
 
 
 class Gather:
-    def __init__(self, row_count, col_count, pieces, own, rows, held, sems, direct=False):
-        self.direct = direct
+    def __init__(self, row_count, col_count, pieces, own, rows, held, sems, packed):
+        self.packed = packed
         self.row_count, self.col_count, self.pieces = row_count, col_count, pieces
         self.own, self.rows, self.held = own, rows, held
-        (self.load, self.send_line, self.recv_line, self.send_row, self.recv_row, self.keep) = sems
+        self.send_line, self.recv_line, self.send_row, self.recv_row, self.keep = sems
         self.me_row, self.me_col = lax.axis_index("row"), lax.axis_index("col")
         self.depth = own.shape[0] // pieces
         self.share = row_count // col_count
@@ -59,26 +59,19 @@
     def part(self, piece):
         return pl.ds(piece * self.depth, self.depth)
 
-    def load_copy(self, piece):
-        return pltpu.make_async_copy(
-            self.own.at[self.part(piece), :],
-            self.held.at[self.me_col, self.part(piece), :],
-            self.load.at[piece],
-        )
-
     def block_ref(self, block, piece, mine):
-        if mine and self.direct:
+        if mine:
             return self.own.at[self.part(piece), :]
         return self.held.at[block, self.part(piece), :]
 
     def block_part(self, block, index, piece, mine):
         columns = pl.ds(index * self.width, self.width)
-        if mine and self.direct:
+        if mine:
             return self.own.at[self.part(piece), columns]
         return self.held.at[block, self.part(piece), columns]
 
     def row_ref(self, owner, target, piece):
-        if not self.direct:
+        if not self.packed:
             return self.rows.at[owner, self.part(piece), :]
         half = self.row_count // 2
         other = lax.rem(owner + target, 2)
@@ -130,8 +123,6 @@
                 self.row_copy(block, index, piece, mine).start()
 
     def begin(self, piece):
-        if not self.direct:
-            self.load_copy(piece).wait()
         for side in range(2):
 
             @pl.when(self.on(side))
@@ -201,7 +192,6 @@
 
 def gather_sems(row_count, col_count, pieces):
     return [
-        pltpu.SemaphoreType.DMA((pieces,)),
         pltpu.SemaphoreType.DMA((2, col_count, pieces)),
         pltpu.SemaphoreType.DMA((2, col_count, pieces)),
         pltpu.SemaphoreType.DMA((col_count, row_count // col_count, pieces)),
@@ -269,85 +259,16 @@
     ]
 
 
-def gather_kernel(row_count, col_count, pieces, with_cols, *refs):
-    own, rows = refs[0], refs[1]
-    rest = refs[2:]
-    columns = None
-    if with_cols:
-        cols, held = rest[0], rest[1]
-        sems, cols_sems = rest[2:8], rest[8:12]
-        columns = Columns(row_count, pieces, own, cols, cols_sems)
-    else:
-        held, sems = rest[0], rest[1:7]
-    gather = Gather(row_count, col_count, pieces, own, rows, held, sems)
-    for piece in range(pieces):
-        gather.load_copy(piece).start()
-    enter(row_count, col_count, gather.me_row, gather.me_col)
-
-    def source(piece):
-        return held.at[gather.me_col, gather.part(piece), :]
-
-    def own_cols(piece):
-        return pltpu.make_async_copy(
-            source(piece), cols.at[gather.me_row, gather.part(piece), :], columns.load.at[piece]
-        )
-
-    def begin(piece):
-        gather.begin(piece)
-        if with_cols:
-            own_cols(piece).start()
-            columns.begin(piece, source(piece))
-
-    for piece in range(min(2, pieces)):
-        begin(piece)
-    for step in range(pieces + col_count - 2):
-        if step + 2 < pieces:
-            begin(step + 2)
-        for hops in range(1, col_count):
-            if 0 <= step - hops + 1 < pieces:
-                gather.arrive(hops, step - hops + 1)
-        if with_cols and step < pieces:
-            columns.arrive(step)
-    for piece in range(pieces):
-        gather.wait_rows(piece)
-        gather.wait_sends(piece)
-        if with_cols:
-            own_cols(piece).wait()
-            columns.finish(piece, source(piece))
-
-
-def gather_pairs(own, row_count, col_count, with_cols, collective_id):
-    depth, width = own.shape
-    pieces = max(1, min(4, depth // 16))
-    rows = jax.ShapeDtypeStruct(
-        (row_count, depth, width * col_count // row_count), own.dtype
-    )
-    cols = jax.ShapeDtypeStruct((row_count, depth, width), own.dtype)
-    out_shape = (rows, cols) if with_cols else (rows,)
-    scratch = [pltpu.VMEM((col_count, depth, width), own.dtype)]
-    scratch += gather_sems(row_count, col_count, pieces)
-    if with_cols:
-        scratch += columns_sems(row_count, pieces)
-    out = pl.pallas_call(
-        functools.partial(gather_kernel, row_count, col_count, pieces, with_cols),
-        out_shape=out_shape,
-        in_specs=[pl.BlockSpec(memory_space=pl.ANY)],
-        out_specs=tuple(pl.BlockSpec(memory_space=pl.ANY) for _ in out_shape),
-        scratch_shapes=scratch,
-        compiler_params=pltpu.CompilerParams(
-            collective_id=collective_id, has_side_effects=True
-        ),
-        name="gather_cols" if with_cols else "gather_rows",
-    )(own)
-    return [item.reshape(row_count * depth, item.shape[2]) for item in out]
-
-
 def dress_kernel(
-    row_count, col_count, pieces, amplitudes, own, held, dressed, table, rows, mine, kept,
+    row_count, col_count, pieces, amplitudes, own, held, held_y, y_rows, y_cols, dressed, table, rows, mine, kept,
     to_partner, from_partner, to_peer, from_peer, chol, table_sem, chol_sem,
     partner_send, partner_recv, peer_send, peer_recv, *sems
 ):
-    gather = Gather(row_count, col_count, pieces, own, rows, held, sems, direct=True)
+    gather = Gather(row_count, col_count, pieces, own, rows, held, sems[:5], True)
+    second = Gather(
+        row_count, col_count, pieces, dressed, y_rows, held_y, sems[5:10], False
+    )
+    columns = Columns(row_count, pieces, dressed, y_cols, sems[10:])
     me_row, depth = gather.me_row, gather.depth
     partner = me_row + 1 - 2 * lax.rem(me_row, 2)
     half = row_count // 2
@@ -435,6 +356,14 @@
             total = chol[piece, :, span].astype(jnp.float32) + total
             dressed[gather.part(piece), span] = total.astype(jnp.bfloat16)
 
+    def own_y(piece):
+        return dressed.at[gather.part(piece), :]
+
+    def own_cols(piece):
+        return pltpu.make_async_copy(
+            own_y(piece), y_cols.at[me_row, gather.part(piece), :], columns.load.at[piece]
+        )
+
     enter(row_count, col_count, gather.me_row, gather.me_col)
     for piece in range(min(2, pieces)):
         gather.begin(piece)
@@ -442,7 +371,7 @@
         table_copy(index).start()
     for piece in range(pieces):
         chol_copy(piece).start()
-    for step in range(pieces + col_count):
+    for step in range(pieces + 2 * col_count - 1):
         if step + 2 < pieces:
             gather.begin(step + 2)
         for hops in range(1, col_count):
@@ -453,14 +382,26 @@
             pair(piece - 1)
         if 0 <= piece - 2 < pieces:
             close(piece - 2)
+            second.begin(piece - 2)
+            own_cols(piece - 2).start()
+            columns.begin(piece - 2, own_y(piece - 2))
         if 0 <= piece < pieces:
             gather.wait_rows(piece)
             if piece == 0:
                 for index in range(split):
                     table_copy(index).wait()
             multiply(piece)
+        for hops in range(1, col_count):
+            if 0 <= step - col_count - hops < pieces:
+                second.arrive(hops, step - col_count - hops)
+        if 0 <= step - col_count - 1 < pieces:
+            columns.arrive(step - col_count - 1)
     for piece in range(pieces):
         gather.wait_sends(piece)
+        second.wait_rows(piece)
+        second.wait_sends(piece)
+        own_cols(piece).wait()
+        columns.finish(piece, own_y(piece))
         if piece >= pieces - 2:
             partner_copy(piece).wait_send()
             for step in range(1, half):
@@ -473,6 +414,7 @@
     depth_piece, half = depth // pieces, row_count // 2
     bf16, f32, dma = jnp.bfloat16, jnp.float32, pltpu.SemaphoreType.DMA
     scratch = [
+        pltpu.VMEM((depth, width), bf16),
         pltpu.VMEM(amplitudes.shape, bf16),
         pltpu.VMEM((pieces, row_count * depth_piece, amplitudes.shape[0]), bf16),
         pltpu.VMEM((half * depth_piece, width), f32),
@@ -488,34 +430,37 @@
         dma((pieces,)),
         dma((pieces, half)),
         dma((pieces, half)),
-    ] + gather_sems(row_count, col_count, pieces)
-    _, dressed = pl.pallas_call(
+    ]
+    scratch += gather_sems(row_count, col_count, pieces) * 2 + columns_sems(row_count, pieces)
+    rows_width = amplitudes.shape[0]
+    _, _, y_rows, y_cols = pl.pallas_call(
         functools.partial(dress_kernel, row_count, col_count, pieces),
         out_shape=(
             jax.ShapeDtypeStruct((col_count, depth, width), bf16),
-            jax.ShapeDtypeStruct((depth, width), bf16),
+            jax.ShapeDtypeStruct((col_count, depth, width), bf16),
+            jax.ShapeDtypeStruct((row_count, depth, rows_width), bf16),
+            jax.ShapeDtypeStruct((row_count, depth, width), bf16),
         ),
         in_specs=[pl.BlockSpec(memory_space=pl.ANY)] * 2,
-        out_specs=(
-            pl.BlockSpec(memory_space=pl.ANY),
-            pl.BlockSpec(memory_space=pltpu.VMEM),
-        ),
+        out_specs=(pl.BlockSpec(memory_space=pl.ANY),) * 4,
         scratch_shapes=scratch,
         compiler_params=pltpu.CompilerParams(
             collective_id=collective_id, has_side_effects=True, vmem_limit_bytes=67043328
         ),
         name="dress",
     )(amplitudes, own)
-    return dressed
+    return (
+        y_rows.reshape(row_count * depth, rows_width),
+        y_cols.reshape(row_count * depth, width),
+    )
 
 
 def local(row_count, col_count, amplitudes, cholesky, occ_index, vir_index, eps_occ, eps_vir):
     row_position = lax.axis_index("row")
     col_position = lax.axis_index("col")
     rows_block, cols_block = amplitudes.shape
-    ydress = dress_pairs(amplitudes, cholesky, row_count, col_count, 0)
+    ydress_rows, ydress_cols = dress_pairs(amplitudes, cholesky, row_count, col_count, 0)
     contract = (((0,), (0,)), ((), ()))
-    ydress_rows, ydress_cols = gather_pairs(ydress, row_count, col_count, True, 1)
     gram = lax.dot_general(
         ydress_rows, ydress_cols, contract, preferred_element_type=jnp.float32
     )

time: 408 us -> 389 us (0.953)
  Pallas kernels: 350 us -> 334 us
    pallas_call x1 -> x0, Pallas kernels: 146 us -> none  [gather_pairs(): pl.pallas_call(functools.partial(gather_kernel, row_count, col_count, pie...]
    pallas_call x1, Pallas kernels: 204 us -> 334 us  [dress_pairs(): pl.pallas_call(functools.partial(dress_kernel, row_count, col_count, piec...]
where the time goes in v3:
time: 389 us
  Pallas kernels  334 us (86%)
  matrix products  48.2 us (12%)
  other arithmetic  5.91 us (2%)
    pallas_call x1, Pallas kernels, dress_pairs(): pl.pallas_call(functools.partial(dress_kernel, row_count, col_count, piec...  334 us
    dot_general x1, matrix products, local(): lax.dot_general(ydress_rows, ydress_cols, contract, preferred_element_typ...  48.2 us

profile of v3, /device:TPU:0, one launch (start us, length us, event | category | flops | bytes accessed | tf_op | source)
XLA Modules:
  0.0 389.2 jit_solution(15717200669142082433)
XLA Ops:
  0.0 0.8 fusion.2
  0.8 0.9 select_reduce_fusion.3
  1.7 3.8 select_reduce_fusion.1
  5.5 0.6 sub.14
  6.1 0.6 sub.15
  6.7 334.2 %dress.1 = (bf16[4,256,4096]{2,1,0:T(8,128)(2,1)}, bf16[4,256,4096]{2,1,0:T(8,128)(2,1)}, bf16[4,256,4096]{2,1,0:T(8,128)(2,1)}, bf16[4,256,4096]{2,1,0:T(8,128)(2,1)}) custom-call(bf16[4096,4096]{1,0:T(8,128)(2,1)} %amplitudes.1, bf16[256,4096]{1,0:T(8,128)(2,1)} %own.1), custom_call_target="tpu_custom_call" | custom-call | tf_op jit(solution)/shard_map/dress/pallas_call | solution.py:436
  341.0 48.2 %fusion.1 = bf16[4096,4096]{1,0:T(8,128)(2,1)} fusion(bf16[4,256,4096]{2,1,0:T(8,128)(2,1)} %get-tuple-element.7, bf16[4,256,4096]{2,1,0:T(8,128)(2,1)} %get-tuple-element.8, f32[4096]{0:T(1024)} %sub.15, f32[4096]{0:T(1024)} %sub.14), kind=kOutput, calls=%fused_computation.2 | convolution fusion | flops 34426847232 | bytes 50364416 | tf_op jit(solution)/shard_map/dot_general | solution.py:464
